TPU v7x, 32 devices: a whole 2x2x4 slice. The times are simulated.
32 devices in a mesh: row: 4 (over z), col: 8 (over y, x, core).
Axes of the slice: x: 2, y: 2, z: 4, core: 2. Of those that a mesh axis runs over, the one named last changes fastest.
Arguments:
- ancestor_pivot: float32 [8, 512, 4, 1024], P(None, 'row', None, 'col'), as said below
- child_pivot: float32 [8, 512, 4, 1024], P(None, 'row', None, 'col'), as said below
- child_panel: float32 [8, 512, 4, 1024], P(None, 'row', None, 'col'), may hold values from -0.09375 to 0.09375
- block_pattern: int32 [32, 32], replicated, may hold values 0 or 1
Outputs:
- child_inverse: float32 [8, 512, 4, 1024], P(None, 'row', None, 'col')
Inputs may be any that keep to these rules, and one draw needn't show every extreme that they name: ancestor_pivot is an exactly symmetric 4096 x 4096 matrix. child_pivot is an exactly symmetric 4096 x 4096 matrix.
All inputs are finite; a program needn't handle non-finite values.
Results may differ from a plain program's by a relative error of at most 0.00005.
Values sent between devices are 32-bit elements; how exact they have to be, the bound alone decides.
A program may use at most 128 MiB of HBM per device.

v0:
```python
import jax
import jax.numpy as jnp
from jax import lax
from jax.sharding import PartitionSpec as P


def column_term(stationary, local_rows, piece):
    shaped = piece.reshape(local_rows, piece.shape[2], piece.shape[3])
    return jnp.einsum(
        "kcl,kn->cln",
        shaped,
        stationary,
        precision=lax.Precision.HIGHEST,
        preferred_element_type=jnp.float32,
    )


def local(ancestor_pivot, child_pivot, child_panel, block_pattern):
    anc_blocks = child_panel.shape[0]
    block_size = child_panel.shape[1]
    col_blocks = child_panel.shape[2]
    anc_col_blocks = ancestor_pivot.shape[2]
    child_rows = child_pivot.shape[0]
    row_count = lax.axis_size("row")
    col_count = lax.axis_size("col")
    row_index = lax.axis_index("row")
    col_index = lax.axis_index("col")
    local_rows = anc_blocks * block_size
    local_cols = col_blocks * block_size
    blocks = block_pattern.reshape(anc_blocks, row_count, col_blocks, col_count)
    local_mask = lax.dynamic_index_in_dim(blocks, row_index, 1, keepdims=False)
    local_mask = lax.dynamic_index_in_dim(local_mask, col_index, 2, keepdims=False)
    masked = child_panel * local_mask.astype(jnp.float32)[:, None, :, None]
    masked_flat = masked.reshape(local_rows, local_cols)
    panel_all = lax.all_gather(masked, "row", axis=1, tiled=True)
    panel_split = panel_all.reshape(anc_col_blocks, col_count * block_size, local_cols)
    segment = lax.all_gather(ancestor_pivot, "col", axis=3, tiled=True)
    length = segment.shape[3]
    weights = segment.reshape(local_rows, anc_col_blocks, length)
    product = jnp.einsum(
        "kcl,cln->kn",
        weights,
        panel_split,
        precision=lax.Precision.HIGHEST,
        preferred_element_type=jnp.float32,
    )
    product_blocks = product.reshape(anc_blocks, block_size, col_blocks, block_size)
    term = column_term(
        masked_flat, local_rows, lax.all_gather(product_blocks, "col", axis=3, tiled=True)
    )
    term = term.reshape(child_rows, row_count, block_size, local_cols)
    term = jnp.transpose(term, (1, 0, 2, 3)).reshape(
        row_count * child_rows * block_size, local_cols
    )
    summed = lax.psum_scatter(term, "row", scatter_dimension=0, tiled=True)
    return child_pivot + summed.reshape(child_rows, block_size, col_blocks, block_size)


def solution(mesh):
    return jax.shard_map(
        local,
        mesh=mesh,
        in_specs=(
            P(None, "row", None, "col"),
            P(None, "row", None, "col"),
            P(None, "row", None, "col"),
            P(),
        ),
        out_specs=P(None, "row", None, "col"),
        check_vma=False,
    )
```

profile of v0, /device:TPU:0, one launch (start us, length us, event | category | flops | bytes accessed | tf_op | source)
XLA Modules:
  0.0 626.5 jit_solution(12353932388971323393)
XLA Ops:
  6.5 0.0 all-gather.4.cloned.1.call-start
  6.5 0.8 reshape.28
  7.4 0.1 constant_dynamic-slice_fusion
  7.4 0.1 copy.15
  7.6 0.1 copy.9
  7.6 3.4 broadcast_multiply_fusion
  11.0 0.0 all-gather.4.cloned.1.call-update
  11.0 0.0 all-gather.6.cloned.1.call-start
  11.1 0.7 all-gather.6.cloned.1.call-update
  11.8 0.0 all-gather.8.cloned.1.call-start
  11.8 151.7 %all-gather.4.cloned.1.call-done = f32[8,512,4,128]{3,2,1,0:T(4,128)} async-done(((f32[8,128,4,128]{3,2,1,0:T(4,128)}), f32[8,512,4,128]{3,2,1,0:T(4,128)}) %all-gather.4.cloned.1.call-update) | async-done | bytes 8388624 | tf_op jit(solution)/shard_map/all_gather | solution.py:35
  163.5 10.5 %reshape.29 = f32[4,1024,512]{2,1,0:T(8,128)} reshape(f32[8,512,4,128]{3,2,1,0:T(4,128)} %all-gather.4.cloned.1.call-done) | data formatting | bytes 16777216 | tf_op jit(solution)/shard_map/reshape | solution.py:36
  174.0 82.6 %all-gather.6.cloned.1.call-done = f32[8,128,4,1024]{3,2,1,0:T(4,128)} async-done(((f32[8,128,4,128]{3,2,1,0:T(4,128)}), f32[8,128,4,1024]{3,2,1,0:T(4,128)}) %all-gather.6.cloned.1.call-update) | async-done | bytes 16777232 | tf_op jit(solution)/shard_map/all_gather | solution.py:37
  256.6 0.0 copy-start.1
  256.6 15.3 %copy.10 = f32[8,128,4,1024]{3,1,0,2:T(8,128)S(1)} copy(f32[8,128,4,1024]{3,2,1,0:T(4,128)} %all-gather.6.cloned.1.call-done) | data formatting | bytes 33554432 | tf_op jit(solution)/shard_map/all_gather | solution.py:37
  272.0 0.0 copy-done.1
  272.0 0.0 copy-start
  272.0 54.8 %convolution_bitcast_fusion.1 = f32[64,8,8,128]{3,1,2,0:T(8,128)S(1)} fusion(f32[4,1024,512]{2,1,0:T(8,128)S(1)} %copy-done.1, f32[1024,4,1024]{2,0,1:T(8,128)S(1)} %bitcast.29), kind=kOutput, calls=%fused_computation.2 | convolution fusion | flops 25769803776 | bytes 27262976 | tf_op jit(solution)/shard_map/kcl,cln->kn/dot_general | solution.py:40
  326.9 1.8 copy.16
  328.6 0.0 all-gather.8.cloned.1.call-update
  328.7 0.0 reduce-scatter.2.cloned.1.call-start
  328.7 0.0 copy-done
  328.7 1.8 reshape.37
  330.6 88.0 %all-gather.8.cloned.1.call-done = f32[8,128,4,1024]{1,0,3,2:T(8,128)} async-done(((f32[8,128,4,128]{1,0,3,2:T(8,128)}), f32[8,128,4,1024]{1,0,3,2:T(8,128)}) %all-gather.8.cloned.1.call-update) | async-done | bytes 16777232 | tf_op jit(solution)/shard_map/all_gather | solution.py:49
  418.5 18.0 %reshape.32 = f32[1024,4,1024]{0,2,1:T(8,128)} reshape(f32[8,128,4,1024]{1,0,3,2:T(8,128)} %all-gather.8.cloned.1.call-done) | data formatting | bytes 33554432 | tf_op jit(solution)/shard_map/reshape | solution.py:8
  436.5 0.0 copy-done.2
  436.5 29.1 %convolution_bitcast_fusion = f32[4,8,128,512]{3,2,0,1:T(8,128)S(1)} fusion(f32[8,4,128,1024]{3,2,1,0:T(8,128)} %bitcast.30, f32[1024,512,1,1]{1,0,2,3:T(8,128)S(1)} %copy-done.2), kind=kOutput, calls=%fused_computation | convolution fusion | flops 25769803776 | bytes 27262976 | tf_op jit(solution)/shard_map/kcl,kn->cln/dot_general | solution.py:9
  465.6 4.2 copy.12
  469.8 0.0 reduce-scatter.2.cloned.1.call-update
  469.9 144.8 %reduce-scatter.2.cloned.1.call-done = f32[1024,512]{1,0:T(8,128)} async-done(((f32[4096,512]{1,0:T(8,128)}), f32[1024,512]{1,0:T(8,128)}) %reduce-scatter.2.cloned.1.call-update) | async-done | bytes 2097168 | tf_op jit(solution)/shard_map/reduce_scatter | solution.py:55
  614.6 1.9 reshape.35
  616.6 3.5 add.19
  (2 shorter events, 0.0 us)
Async XLA Ops:
  6.5 157.0 %all-gather.4.cloned.1.call-start = ((), (), s32[]{:S(2)}) async-start(), calls=%async_computation.1 | async-start | bytes 10485760 | tf_op jit(solution)/shard_map/all_gather | solution.py:35
  11.0 245.6 %all-gather.6.cloned.1.call-start = ((), (), s32[]{:S(2)}) async-start(), calls=%async_computation.2 | async-start | bytes 18874368 | tf_op jit(solution)/shard_map/all_gather | solution.py:37
  11.8 406.8 %all-gather.8.cloned.1.call-start = ((), (), s32[]{:S(2)}) async-start(), calls=%async_computation.3 | async-start | bytes 18874368 | tf_op jit(solution)/shard_map/all_gather | solution.py:49
  256.6 15.4 %copy-start.1 = (f32[4,1024,512]{2,1,0:T(8,128)S(1)}, f32[4,1024,512]{2,1,0:T(8,128)}, u32[]{:S(2)}) copy-start(f32[4,1024,512]{2,1,0:T(8,128)} %reshape.29) | copy-start | bytes 25165828
  272.0 56.7 %copy-start = (f32[8,128,4,128]{3,2,1,0:T(4,128)S(1)}, f32[8,128,4,128]{3,2,1,0:T(4,128)}, u32[]{:S(2)}) copy-start(f32[8,128,4,128]{3,2,1,0:T(4,128)} %broadcast_multiply_fusion) | copy-start | bytes 6291460
  328.7 286.0 %reduce-scatter.2.cloned.1.call-start = ((), (), s32[]{:S(2)}) async-start(), calls=%async_computation.4 | async-start | bytes 10485760 | tf_op jit(solution)/shard_map/reduce_scatter | solution.py:55
  330.6 106.0 %copy-start.2 = (f32[1024,512,1,1]{1,0,2,3:T(8,128)S(1)}, f32[1024,512,1,1]{1,0,2,3:T(8,128)}, u32[]{:S(2)}) copy-start(f32[1024,512,1,1]{1,0,2,3:T(8,128)} %reshape.37) | copy-start | bytes 6291460
Sparse Core Ops, SparseCore 0:
  11.1 152.3 all-gather.3
  165.4 91.1 all-gather.5
  328.8 89.7 all-gather.7
  470.0 144.6 reduce-scatter.1
where the time goes:
time: 627 us
  waiting for transfers between devices  468 us (75%)
  matrix products  83.9 us (13%)
  local copies, waits for them, and re-layouts  54.7 us (9%)
  between operations  13.2 us (2%)
  other arithmetic  6.82 us (1%)
    all_gather x1, waiting for transfers between devices, local(): panel_all = lax.all_gather(masked, 'row', axis=1, tiled=True)  152 us
    reduce_scatter x1, waiting for transfers between devices, local(): summed = lax.psum_scatter(term, 'row', scatter_dimension=0, tiled=True)  145 us
    all_gather x1, waiting for transfers between devices, local(): lax.all_gather(product_blocks, 'col', axis=3, tiled=True)  88 us
    all_gather x1, waiting for transfers between devices, local(): segment = lax.all_gather(ancestor_pivot, 'col', axis=3, tiled=True)  82.6 us
    dot_general x1, matrix products, local(): jnp.einsum('kcl,cln->kn', weights, panel_split, precision=lax.Precision.H...  54.8 us
    dot_general x1, matrix products, column_term(): jnp.einsum('kcl,kn->cln', shaped, stationary, precision=lax.Precision.HIG...  29.1 us
    reshape x1, local copies, waits for them, and re-layouts, column_term(): shaped = piece.reshape(local_rows, piece.shape[2], piece.shape[3])  18 us
    all_gather x1, local copies, waits for them, and re-layouts, local(): segment = lax.all_gather(ancestor_pivot, 'col', axis=3, tiled=True)  15.3 us
  transfers between devices with their start and end apart: 4, of which 4 were waited for; matrix products, arithmetic and copies ran while one was open for 2% of the time, Pallas kernels for 0%

commit v1 on v0

--- a/solution.py
+++ b/solution.py
@@ -32,7 +32,12 @@
     local_mask = lax.dynamic_index_in_dim(local_mask, col_index, 2, keepdims=False)
     masked = child_panel * local_mask.astype(jnp.float32)[:, None, :, None]
     masked_flat = masked.reshape(local_rows, local_cols)
-    panel_all = lax.all_gather(masked, "row", axis=1, tiled=True)
+    ring = [masked]
+    for hop in range(3):
+        ring.append(lax.ppermute(ring[-1], "row", [(dev, (dev + 1) % 4) for dev in range(4)]))
+    panel_all = jnp.roll(
+        jnp.concatenate(ring[::-1], axis=1), (lax.axis_index("row") + 1) * ring[0].shape[1], axis=1
+    )
     panel_split = panel_all.reshape(anc_col_blocks, col_count * block_size, local_cols)
     segment = lax.all_gather(ancestor_pivot, "col", axis=3, tiled=True)
     length = segment.shape[3]

time: 627 us -> 567 us (0.904)
  waiting for transfers between devices: 468 us -> 376 us
  local copies, waits for them, and re-layouts: 54.7 us -> 80.8 us
    all_gather x1 -> x0, waiting for transfers between devices: 152 us -> none  [local(): panel_all = lax.all_gather(masked, 'row', axis=1, tiled=True)]
    ppermute x0 -> x3, waiting for transfers between devices: none -> 144 us  [local(): lax.ppermute(ring[-1], 'row', [(dev, (dev + 1) % 4) for dev in range(4)])]
    all_gather x1, waiting for transfers between devices: 82.6 us -> 0.01 us  [local(): segment = lax.all_gather(ancestor_pivot, 'col', axis=3, tiled=True)]
    unnamed x8 -> x22, local copies, waits for them, and re-layouts: 1.91 us -> 20.9 us
    dynamic_slice x0 -> x1, local copies, waits for them, and re-layouts: none -> 7.21 us  [local(): jnp.roll(jnp.concatenate(ring[::-1], axis=1), (lax.axis_index('row') + 1)...]
  transfers between devices with their start and end apart: 4 -> 6, of which waited for: 4 -> 5; matrix products, arithmetic and copies ran while one was open for 2% -> 8% of each run, Pallas kernels for 0% -> 0%
where the time goes in v1:
time: 567 us; the launch traced here: 566 us
  waiting for transfers between devices  376 us (66%)
  matrix products  83.9 us (15%)
  local copies, waits for them, and re-layouts  80.8 us (14%)
  between operations  13.2 us (2%)
  other arithmetic  9.15 us (2%)
    reduce_scatter x1, waiting for transfers between devices, local(): summed = lax.psum_scatter(term, 'row', scatter_dimension=0, tiled=True)  145 us
    ppermute x3, waiting for transfers between devices, local(): lax.ppermute(ring[-1], 'row', [(dev, (dev + 1) % 4) for dev in range(4)])  144 us
    all_gather x1, waiting for transfers between devices, local(): lax.all_gather(product_blocks, 'col', axis=3, tiled=True)  85.7 us
    dot_general x1, matrix products, local(): jnp.einsum('kcl,cln->kn', weights, panel_split, precision=lax.Precision.H...  54.8 us
    dot_general x1, matrix products, column_term(): jnp.einsum('kcl,kn->cln', shaped, stationary, precision=lax.Precision.HIG...  29.1 us
    unnamed x22, local copies, waits for them, and re-layouts  20.9 us
    reshape x1, local copies, waits for them, and re-layouts, column_term(): shaped = piece.reshape(local_rows, piece.shape[2], piece.shape[3])  18 us
    all_gather x1, local copies, waits for them, and re-layouts, local(): segment = lax.all_gather(ancestor_pivot, 'col', axis=3, tiled=True)  15.3 us
  transfers between devices with their start and end apart: 6, of which 5 were waited for; matrix products, arithmetic and copies ran while one was open for 8% of the time, Pallas kernels for 0%

profile of v1, /device:TPU:0, one launch (start us, length us, event | category | flops | bytes accessed | tf_op | source)
XLA Modules:
  0.0 565.9 jit_solution(16264722511990331249)
XLA Ops:
  6.5 0.7 all-gather.3.cloned.1.call-update
  7.3 0.8 reshape.28
  8.2 0.1 copy.15
  8.3 0.1 copy.9
  8.4 2.2 broadcast_multiply_fusion
  10.7 1.4 copy-done.1
  12.0 3.1 collective-permute-start
  15.1 47.7 %collective-permute-done = f32[8,128,4,128]{3,2,1,0:T(4,128)S(1)} collective-permute-done((f32[8,128,4,128]{3,2,1,0:T(4,128)S(1)}, f32[8,128,4,128]{3,2,1,0:T(4,128)S(1)}, u32[]{:S(2)}, u32[]{:S(2)}) %collective-permute-start) | collective-permute-done | bytes 2097184 | tf_op jit(solution)/shard_map/ppermute | solution.py:37
  62.7 1.3 copy-done.4
  64.0 48.7 %collective-permute-done.1 = f32[8,128,4,128]{3,2,1,0:T(4,128)} collective-permute-done((f32[8,128,4,128]{3,2,1,0:T(4,128)S(1)}, f32[8,128,4,128]{3,2,1,0:T(4,128)}, u32[]{:S(2)}, u32[]{:S(2)}) %collective-permute-start.1) | collective-permute-done | bytes 2097184 | tf_op jit(solution)/shard_map/ppermute | solution.py:37
  112.7 48.0 %collective-permute-done.2 = f32[8,128,4,128]{3,2,1,0:T(4,128)} collective-permute-done((f32[8,128,4,128]{3,2,1,0:T(4,128)}, f32[8,128,4,128]{3,2,1,0:T(4,128)}, u32[]{:S(2)}, u32[]{:S(2)}) %collective-permute-start.2) | collective-permute-done | bytes 2097184 | tf_op jit(solution)/shard_map/ppermute | solution.py:37
  160.8 3.3 constant_dynamic-update-slice_fusion.7
  164.1 3.3 constant_dynamic-update-slice_fusion.6
  167.4 1.6 constant_dynamic-update-slice_fusion.5
  169.0 1.7 constant_dynamic-update-slice_fusion.4
  170.7 3.2 constant_dynamic-update-slice_fusion.3
  174.0 3.2 constant_dynamic-update-slice_fusion.2
  177.2 1.7 constant_dynamic-update-slice_fusion.1
  178.9 1.7 constant_dynamic-update-slice_fusion
  180.6 7.2 %constant_dynamic-slice_fusion = f32[8,512,4,128]{3,2,1,0:T(4,128)} fusion(f32[8,1024,4,128]{3,2,1,0:T(4,128)} %constant_dynamic-update-slice_fusion, s32[]{:T(128)S(6)} %select_n.30), kind=kLoop, calls=%fused_computation.13 | loop fusion | bytes 16777220 | tf_op jit(solution)/shard_map/jit(_roll_dynamic)/dynamic_slice | solution.py:38
  187.8 10.3 %reshape.29 = f32[4,1024,512]{2,1,0:T(8,128)} reshape(f32[8,512,4,128]{3,2,1,0:T(4,128)} %constant_dynamic-slice_fusion) | data formatting | bytes 16777216 | tf_op jit(solution)/shard_map/reshape | solution.py:41
  198.2 15.3 %copy.10 = f32[8,128,4,1024]{3,1,0,2:T(8,128)S(1)} copy(f32[8,128,4,1024]{3,2,1,0:T(4,128)} %all-gather.3.cloned.1.call-done) | data formatting | bytes 33554432 | tf_op jit(solution)/shard_map/all_gather | solution.py:42
  213.5 54.8 %convolution_bitcast_fusion.1 = f32[64,8,8,128]{3,1,2,0:T(8,128)S(1)} fusion(f32[4,1024,512]{2,1,0:T(8,128)S(1)} %copy-done.3, f32[1024,4,1024]{2,0,1:T(8,128)S(1)} %bitcast.29), kind=kOutput, calls=%fused_computation.2 | convolution fusion | flops 25769803776 | bytes 27262976 | tf_op jit(solution)/shard_map/kcl,cln->kn/dot_general | solution.py:45
  268.4 1.8 copy.16
  270.3 1.9 reshape.37
  272.1 85.7 %all-gather.5.cloned.1.call-done = f32[8,128,4,1024]{1,0,3,2:T(8,128)} async-done(((f32[8,128,4,128]{1,0,3,2:T(8,128)}), f32[8,128,4,1024]{1,0,3,2:T(8,128)}) %all-gather.5.cloned.1.call-update) | async-done | bytes 16777232 | tf_op jit(solution)/shard_map/all_gather | solution.py:54
  357.8 18.0 %reshape.32 = f32[1024,4,1024]{0,2,1:T(8,128)} reshape(f32[8,128,4,1024]{1,0,3,2:T(8,128)} %all-gather.5.cloned.1.call-done) | data formatting | bytes 33554432 | tf_op jit(solution)/shard_map/reshape | solution.py:8
  375.8 29.1 %convolution_bitcast_fusion = f32[4,8,128,512]{3,2,0,1:T(8,128)S(1)} fusion(f32[8,4,128,1024]{3,2,1,0:T(8,128)} %bitcast.30, f32[1024,512,1,1]{1,0,2,3:T(8,128)S(1)} %copy-done.6), kind=kOutput, calls=%fused_computation | convolution fusion | flops 25769803776 | bytes 27262976 | tf_op jit(solution)/shard_map/kcl,kn->cln/dot_general | solution.py:9
  404.9 4.2 copy.12
  409.2 144.8 %reduce-scatter.2.cloned.1.call-done = f32[1024,512]{1,0:T(8,128)} async-done(((f32[4096,512]{1,0:T(8,128)}), f32[1024,512]{1,0:T(8,128)}) %reduce-scatter.2.cloned.1.call-update) | async-done | bytes 2097168 | tf_op jit(solution)/shard_map/reduce_scatter | solution.py:60
  553.9 1.9 reshape.35
  555.9 3.5 add.35
  (22 shorter events, 0.2 us)
Async XLA Ops:
  6.5 191.6 %all-gather.3.cloned.1.call-start = ((), (), s32[]{:S(2)}) async-start(), calls=%async_computation.1 | async-start | bytes 18874368 | tf_op jit(solution)/shard_map/all_gather | solution.py:42
  7.3 350.6 %all-gather.5.cloned.1.call-start = ((), (), s32[]{:S(2)}) async-start(), calls=%async_computation.2 | async-start | bytes 18874368 | tf_op jit(solution)/shard_map/all_gather | solution.py:54
  8.4 160.6 %copy-start = (f32[8,128,4,128]{3,2,1,0:T(4,128)S(1)}, f32[8,128,4,128]{3,2,1,0:T(4,128)}, u32[]{:S(2)}) copy-start(f32[8,128,4,128]{3,2,1,0:T(4,128)} %param.6) | copy-start | bytes 6291460
  10.6 1.4 copy-start.1
  12.0 50.7 %collective-permute-start = (f32[8,128,4,128]{3,2,1,0:T(4,128)S(1)}, f32[8,128,4,128]{3,2,1,0:T(4,128)S(1)}, u32[]{:S(2)}, u32[]{:S(2)}) collective-permute-start(f32[8,128,4,128]{3,2,1,0:T(4,128)S(1)} %broadcast_multiply_fusion), channel_id=1, source_target_pairs={{0,8},{8,16},{16,24},{24,0},{1,9},{9,17},{17,25},{25,1},{2,10},{10... | collective-permute-start | bytes 6291464 | tf_op jit(solution)/shard_map/ppermute | solution.py:37
  62.7 1.3 copy-start.4
  64.0 48.7 %collective-permute-start.1 = (f32[8,128,4,128]{3,2,1,0:T(4,128)S(1)}, f32[8,128,4,128]{3,2,1,0:T(4,128)}, u32[]{:S(2)}, u32[]{:S(2)}) collective-permute-start(f32[8,128,4,128]{3,2,1,0:T(4,128)S(1)} %collective-permute-done), channel_id=1, source_target_pairs={{0,8},{8,16},{16,24},{24,0},{1,9},{9,17},{17,25},{25,1},{2,10},{10... | collective-permute-start | bytes 6291464 | tf_op jit(solution)/shard_map/ppermute | solution.py:37
  112.7 48.1 %collective-permute-start.2 = (f32[8,128,4,128]{3,2,1,0:T(4,128)}, f32[8,128,4,128]{3,2,1,0:T(4,128)}, u32[]{:S(2)}, u32[]{:S(2)}) collective-permute-start(f32[8,128,4,128]{3,2,1,0:T(4,128)} %collective-permute-done.1), channel_id=1, source_target_pairs={{0,8},{8,16},{16,24},{24,0},{1,9},{9,17},{17,25},{25,1},{2,10},{10... | collective-permute-start | bytes 6291464 | tf_op jit(solution)/shard_map/ppermute | solution.py:37
  112.7 54.6 %copy-start.5 = (f32[8,128,4,128]{3,2,1,0:T(4,128)S(1)}, f32[8,128,4,128]{3,2,1,0:T(4,128)}, u32[]{:S(2)}) copy-start(f32[8,128,4,128]{3,2,1,0:T(4,128)} %copy-done.4) | copy-start | bytes 6291460
  198.2 15.4 %copy-start.3 = (f32[4,1024,512]{2,1,0:T(8,128)S(1)}, f32[4,1024,512]{2,1,0:T(8,128)}, u32[]{:S(2)}) copy-start(f32[4,1024,512]{2,1,0:T(8,128)} %reshape.29) | copy-start | bytes 25165828
  213.5 56.7 %copy-start.2 = (f32[8,128,4,128]{3,2,1,0:T(4,128)S(1)}, f32[8,128,4,128]{3,2,1,0:T(4,128)}, u32[]{:S(2)}) copy-start(f32[8,128,4,128]{3,2,1,0:T(4,128)} %copy-done.1) | copy-start | bytes 6291460
  270.2 283.8 %reduce-scatter.2.cloned.1.call-start = ((), (), s32[]{:S(2)}) async-start(), calls=%async_computation.3 | async-start | bytes 10485760 | tf_op jit(solution)/shard_map/reduce_scatter | solution.py:60
  272.1 103.7 %copy-start.6 = (f32[1024,512,1,1]{1,0,2,3:T(8,128)S(1)}, f32[1024,512,1,1]{1,0,2,3:T(8,128)}, u32[]{:S(2)}) copy-start(f32[1024,512,1,1]{1,0,2,3:T(8,128)} %reshape.37) | copy-start | bytes 6291460
Sparse Core Ops, SparseCore 0:
  9.2 95.7 all-gather.2
  270.3 87.4 all-gather.4
  409.3 144.6 reduce-scatter.1
